TPU v7x, 256 devices: a whole 4x4x8 slice. The times are simulated.
256 devices in a mesh: req: 16 (over z_hi, x), mp: 16 (over z_lo, y, core).
Axes of the slice: x: 4, y: 4, z: 8 (z_hi: 4, z_lo: 2; z = z_hi * 2 + z_lo), core: 2. Of those that a mesh axis runs over, the one named last changes fastest.
Arguments:
- queries: bfloat16 [2048, 4096], P('req', 'mp'), may hold values from -6 to 6
- suffix_kv: bfloat16 [2, 2048, 4096], P(None, 'req', 'mp'), may hold values from -6 to 6
- prefix_kv: bfloat16 [2, 8192, 4096], P(None, 'req', 'mp'), may hold values from -6 to 6
- resid: bfloat16 [2048, 4096], P('req', 'mp'), may hold values from -6 to 6
- ln_gain: float32 [4096], replicated, may hold values from 0.1 to 1.9
- out_weight: bfloat16 [4096, 4096], P('mp'), may hold values from -0.125 to 0.125
- up_weight: bfloat16 [4096, 8192], P(None, 'mp'), may hold values from -0.09375 to 0.09375
- down_weight: bfloat16 [8192, 4096], P('mp'), may hold values from -0.09375 to 0.09375
- lengths: int32 [16], replicated, may hold values from 1 to 128, 1024 in all
- req_group: int32 [16], replicated, may hold values from 0 to 3, as said below
- prefix_owner: int32 [16], replicated, may hold values from 0 to 15, as said below
Outputs:
- attended: bfloat16 [2048, 4096], P('req', 'mp')
- layer_out: bfloat16 [2048, 4096], P('req', 'mp')
Inputs may be any that keep to these rules, and one draw needn't show every extreme that they name: `req_group`: each of the 4 groups holds exactly 4 requests. `prefix_owner`: a permutation: every logical block is held by exactly one stored block.
All inputs are finite; a program needn't handle non-finite values.
Results may differ from a plain program's by a relative error of at most 0.029.
Values may be sent and summed in bfloat16 or wider, within the bound.
A program may use at most 128 MiB of HBM per device.

v0:
```python
import jax
import jax.numpy as jnp
from jax import lax
from jax.sharding import PartitionSpec as P

H = 32
DH = 128
KB = 512
S_MAX = 128
P_SIZE = 2048
very_negative = -1e30


def block_partial(query_rows, key_rows, value_rows, query_pos, key_pos, allowed, slopes, shared):
    if shared:
        score_form = "rqhd,khd->rqhk"
        value_form = "rqhk,khd->rqhd"
    else:
        score_form = "rqhd,rkhd->rqhk"
        value_form = "rqhk,rkhd->rqhd"
    scores = jnp.einsum(
        score_form, query_rows, key_rows, preferred_element_type=jnp.float32
    ) * float(DH) ** (-0.5)
    distance = (query_pos[:, None, None] - key_pos[None, None, :]).astype(jnp.float32)
    scores = scores - slopes[None, :, None] * distance
    masked = jnp.where(allowed, scores, very_negative)
    maxima = jnp.max(masked, axis=-1)
    weights = jnp.where(allowed, jnp.exp(masked - maxima[..., None]), 0.0)
    totals = jnp.sum(weights, axis=-1)
    rounded = weights.astype(jnp.bfloat16)
    weighted = jnp.einsum(value_form, rounded, value_rows, preferred_element_type=jnp.float32)
    return (weighted, maxima, totals)


def combine(first_part, second_part):
    peak_max = jnp.maximum(first_part[1], second_part[1])
    scale_first = jnp.exp(first_part[1] - peak_max)
    scale_second = jnp.exp(second_part[1] - peak_max)
    weighted = first_part[0] * scale_first[..., None] + second_part[0] * scale_second[..., None]
    return (weighted, peak_max, first_part[2] * scale_first + second_part[2] * scale_second)


def shards(
    queries,
    suffix_kv,
    prefix_kv,
    resid,
    ln_gain,
    out_weight,
    up_weight,
    down_weight,
    lengths,
    req_group,
    prefix_owner,
):
    row_count = queries.shape[0]
    local_req = row_count // S_MAX
    columns = queries.shape[1]
    head_count = columns // DH
    per_group = P_SIZE // KB
    first_req = lax.axis_index("req") * local_req
    col_start = lax.axis_index("mp") * columns
    my_len = lax.dynamic_slice_in_dim(lengths, first_req, local_req)
    my_group = lax.dynamic_slice_in_dim(req_group, first_req, local_req)
    head_ids = (lax.axis_index("mp") * head_count + jnp.arange(head_count)).astype(jnp.float32)
    slopes = jnp.power(2.0, -8.0 * (head_ids + 1.0) / H)
    my_query = queries.reshape(local_req, S_MAX, head_count, DH)
    suffix_local = suffix_kv.reshape(2, local_req, S_MAX, head_count, DH)
    offsets = jnp.arange(S_MAX)
    query_pos = P_SIZE + offsets
    allowed = (offsets[None, None, :] <= offsets[None, :, None]) & (
        offsets[None, None, :] < my_len[:, None, None]
    )
    own_part = block_partial(
        my_query,
        suffix_local[0],
        suffix_local[1],
        query_pos,
        query_pos,
        allowed[:, :, None, :],
        slopes,
        False,
    )
    key_offsets = jnp.arange(KB)
    shard_piece = lax.all_gather(prefix_kv, "req", axis=1, tiled=True)
    block_total = shard_piece.shape[1] // KB
    blocks_here = shard_piece.reshape(2, block_total, KB, head_count, DH)

    def fold_step(block_index, inner_state):
        logical = prefix_owner[block_index]
        same_group = my_group == logical // per_group
        base_pos = logical % per_group * KB

        def attend_block(state_in):
            fresh = block_partial(
                my_query,
                blocks_here[0, block_index],
                blocks_here[1, block_index],
                query_pos,
                base_pos + key_offsets,
                same_group[:, None, None, None],
                slopes,
                True,
            )
            return combine(state_in, fresh)

        return lax.cond(jnp.any(same_group), attend_block, lambda state_in: state_in, inner_state)

    result = lax.fori_loop(0, block_total, fold_step, own_part)
    outcome = result[0] / result[2][..., None]
    live_mask = offsets[None, :] < my_len[:, None]
    attended = (
        jnp.where(live_mask[:, :, None, None], outcome, 0.0)
        .astype(jnp.bfloat16)
        .reshape(row_count, columns)
    )
    head_term = jnp.dot(attended, out_weight, preferred_element_type=jnp.float32)
    own_columns = lax.dynamic_slice_in_dim(head_term, col_start, columns, 1) + resid.astype(
        jnp.float32
    )
    head_term = lax.dynamic_update_slice_in_dim(head_term, own_columns, col_start, 1)
    mixed_rows = lax.psum(head_term.astype(jnp.bfloat16), "mp").astype(jnp.float32)
    row_mean = jnp.mean(mixed_rows, axis=1, keepdims=True)
    centered = mixed_rows - row_mean
    variance = jnp.mean(centered * centered, axis=1, keepdims=True)
    normed = (centered * lax.rsqrt(variance + 1e-05) * ln_gain).astype(jnp.bfloat16)
    hidden = jax.nn.gelu(
        jnp.dot(normed, up_weight, preferred_element_type=jnp.float32), approximate=False
    ).astype(jnp.bfloat16)
    projected = jnp.dot(hidden, down_weight, preferred_element_type=jnp.float32)
    update = lax.psum_scatter(
        projected.astype(jnp.bfloat16), "mp", scatter_dimension=1, tiled=True
    ).astype(jnp.float32)
    mixed_own = lax.dynamic_slice_in_dim(mixed_rows, col_start, columns, 1)
    layer_out = jnp.where(live_mask.reshape(row_count)[:, None], mixed_own + update, 0.0).astype(
        jnp.bfloat16
    )
    return (attended, layer_out)


def solution(mesh):
    placed = (
        P("req", "mp"),
        P(None, "req", "mp"),
        P(None, "req", "mp"),
        P("req", "mp"),
        P(),
        P("mp", None),
        P(None, "mp"),
        P("mp", None),
        P(),
        P(),
        P(),
    )
    return jax.shard_map(
        shards,
        mesh=mesh,
        in_specs=placed,
        out_specs=(P("req", "mp"), P("req", "mp")),
        check_vma=False,
    )
```

profile of v0, /device:TPU:6, one launch (start us, length us, event | category | flops | bytes accessed | tf_op | source)
XLA Modules:
  0.0 440.7 jit_solution(7493433449119299911)
XLA Ops:
  7.2 0.7 all-gather.2.cloned.1.call-update
  8.0 1.2 dynamic_slice.35
  9.2 1.2 dynamic_slice.34
  10.4 0.9 copy.28
  11.5 0.9 fusion.121
  13.4 1.1 fusion.122
  14.9 107.0 %all-gather.2.cloned.1.call-done = bf16[2,8192,256]{2,1,0:T(8,128)(2,1)} async-done(((bf16[2,512,256]{2,1,0:T(8,128)(2,1)}), bf16[2,8192,256]{2,1,0:T(8,128)(2,1)}) %all-gather.2.cloned.1.call-update) | async-done | bytes 8388624 | tf_op jit(solution)/shard_map/all_gather | solution.py:85
  121.9 12.5 %reshape.277 = bf16[2,16,512,2,128]{4,3,2,1,0:T(2,128)(2,1)} reshape(bf16[2,8192,256]{2,1,0:T(8,128)(2,1)} %all-gather.2.cloned.1.call-done) | data formatting | bytes 16777216 | tf_op jit(solution)/shard_map/reshape | solution.py:87
  134.4 8.8 %copy.30 = bf16[2,16,512,2,128]{4,2,3,1,0:T(8,128)(2,1)} copy(bf16[2,16,512,2,128]{4,3,2,1,0:T(2,128)(2,1)} %reshape.277) | data formatting | bytes 16777216
  143.2 79.0 %while.20 = (s32[]{:T(128)}, f32[1,128,2,128]{1,3,2,0:T(8,128)S(1)}, f32[1,128,2]{1,2,0:T(2,128)S(1)}, f32[1,128,2]{1,2,0:T(2,128)S(1)}, s32[16]{0:T(128)S(1)}, ...) while((s32[]{:T(128)}, ...), condition=%wide.region_7.8_spmd.clone, body=%wide.region_2.7_spmd.clone.sunk | while | flops 68782248 | bytes 2980505 | solution.py:109
  147.0 0.6 dynamic_slice.54
  150.7 4.7 %conditional.3 = ((f32[1,128,2,128]{1,3,2,0:T(8,128)S(1)}, f32[1,128,2]{1,2,0:T(2,128)S(1)}, f32[1,128,2]{1,2,0:T(2,128)S(1)})) conditional(s32[]{:T(128)} %bitcast.111, (f32[1,128,2,128]{1,3,2,0:T(8,128)S(1)}, f32[1,128,2]{1,2,0:T(2,128)S(1)}, f32[1,128,2]{1,2,0:T(2,128)S(1)}) %tuple.96, (pred[1]{0:T(512)(128)(4,1)}, s32[]{:T(128)}, ...), branch_computations={%region_3.3_spmd, %region_4.6_spmd.clone} | conditional | flops 68782224 | bytes 2977504 | solution.py:107
  152.8 1.2 fusion.120
  154.1 1.3 fusion.10
  174.2 4.7 %conditional.3 = ((f32[1,128,2,128]{1,3,2,0:T(8,128)S(1)}, f32[1,128,2]{1,2,0:T(2,128)S(1)}, f32[1,128,2]{1,2,0:T(2,128)S(1)})) conditional(s32[]{:T(128)} %bitcast.111, (f32[1,128,2,128]{1,3,2,0:T(8,128)S(1)}, f32[1,128,2]{1,2,0:T(2,128)S(1)}, f32[1,128,2]{1,2,0:T(2,128)S(1)}) %tuple.96, (pred[1]{0:T(512)(128)(4,1)}, s32[]{:T(128)}, ...), branch_computations={%region_3.3_spmd, %region_4.6_spmd.clone} | conditional | flops 68782224 | bytes 2977504 | solution.py:107
  176.3 1.2 fusion.120
  177.7 1.3 fusion.10
  190.2 4.7 %conditional.3 = ((f32[1,128,2,128]{1,3,2,0:T(8,128)S(1)}, f32[1,128,2]{1,2,0:T(2,128)S(1)}, f32[1,128,2]{1,2,0:T(2,128)S(1)})) conditional(s32[]{:T(128)} %bitcast.111, (f32[1,128,2,128]{1,3,2,0:T(8,128)S(1)}, f32[1,128,2]{1,2,0:T(2,128)S(1)}, f32[1,128,2]{1,2,0:T(2,128)S(1)}) %tuple.96, (pred[1]{0:T(512)(128)(4,1)}, s32[]{:T(128)}, ...), branch_computations={%region_3.3_spmd, %region_4.6_spmd.clone} | conditional | flops 68782224 | bytes 2977504 | solution.py:107
  192.3 1.2 fusion.120
  193.6 1.3 fusion.10
  217.5 4.7 %conditional.3 = ((f32[1,128,2,128]{1,3,2,0:T(8,128)S(1)}, f32[1,128,2]{1,2,0:T(2,128)S(1)}, f32[1,128,2]{1,2,0:T(2,128)S(1)})) conditional(s32[]{:T(128)} %bitcast.111, (f32[1,128,2,128]{1,3,2,0:T(8,128)S(1)}, f32[1,128,2]{1,2,0:T(2,128)S(1)}, f32[1,128,2]{1,2,0:T(2,128)S(1)}) %tuple.96, (pred[1]{0:T(512)(128)(4,1)}, s32[]{:T(128)}, ...), branch_computations={%region_3.3_spmd, %region_4.6_spmd.clone} | conditional | flops 68782224 | bytes 2977504 | solution.py:107
  219.5 1.2 fusion.120
  220.9 1.3 fusion.10
  223.1 1.2 convert_element_type.80
  224.3 132.2 %all-reduce.2.cloned.1.call-done = bf16[128,4096]{1,0:T(8,128)(2,1)} async-done(((bf16[128,4096]{1,0:T(8,128)(2,1)}), bf16[128,4096]{1,0:T(8,128)(2,1)}) %all-reduce.2.cloned.1.call-update) | async-done | bytes 1048592 | tf_op jit(solution)/shard_map/psum | solution.py:122
  356.5 1.5 convert_reduce_fusion
  358.1 1.7 multiply_reduce_fusion
  359.8 6.4 %convolution_convert_fusion = bf16[128,4096]{1,0:T(8,128)(2,1)} fusion(bf16[512,4096]{1,0:T(8,128)(2,1)} %param.22, bf16[4096,512]{1,0:T(8,128)(2,1)} %param.21, bf16[128,4096]{1,0:T(8,128)(2,1)S(1)} %copy-done.1, f32[4096]{0:T(1024)S(1)} %copy-done.3, f32[128]{0:T(128)S(1)} %add_rsqrt_fusion, f32[128]{0:T(128)S(1)} %broadcast_multiply_fusion), kind=kOutput, calls=%fused_computation.40 | convolution fusion | flops 1081147392 | bytes 10503168 | tf_op jit(solution)/shard_map/dot_general | solution.py:130
  366.2 0.7 copy.32
  367.0 1.6 convert_element_type.81
  368.5 63.9 %reduce-scatter.2.cloned.1.call-done = bf16[128,256]{1,0:T(8,128)(2,1)} async-done(((bf16[128,4096]{1,0:T(8,128)(2,1)}), bf16[128,256]{1,0:T(8,128)(2,1)}) %reduce-scatter.2.cloned.1.call-update) | async-done | bytes 65552 | tf_op jit(solution)/shard_map/reduce_scatter | solution.py:131
  432.5 1.7 select_convert_fusion
  (138 shorter events, 13.0 us)
Async XLA Ops:
  7.2 215.1 %copy-start = (bf16[256,4096]{1,0:T(8,128)(2,1)S(1)}, bf16[256,4096]{1,0:T(8,128)(2,1)}, u32[]{:S(2)}) copy-start(bf16[256,4096]{1,0:T(8,128)(2,1)} %param.20) | copy-start | bytes 6291460
  7.2 114.7 %all-gather.2.cloned.1.call-start = ((), (), s32[]{:S(2)}) async-start(), calls=%async_computation.1 | async-start | bytes 8912896 | tf_op jit(solution)/shard_map/all_gather | solution.py:85
  7.9 348.6 %all-reduce.2.cloned.1.call-start = ((), (), s32[]{:S(2)}) async-start(), calls=%async_computation.2 | async-start | bytes 2097152 | tf_op jit(solution)/shard_map/psum | solution.py:122
  134.4 8.8 %copy-start.4 = (s32[16]{0:T(128)S(1)}, s32[16]{0:T(128)}, u32[]{:S(2)}) copy-start(s32[16]{0:T(128)} %param.25) | copy-start | bytes 196
  222.2 0.8 copy-start.2
  224.3 135.5 %copy-start.3 = (f32[4096]{0:T(1024)S(1)}, f32[4096]{0:T(1024)}, u32[]{:S(2)}) copy-start(f32[4096]{0:T(1024)} %param.19) | copy-start | bytes 49156
  224.3 208.2 %reduce-scatter.2.cloned.1.call-start = ((), (), s32[]{:S(2)}) async-start(), calls=%async_computation.3 | async-start | bytes 1114112 | tf_op jit(solution)/shard_map/reduce_scatter | solution.py:131
  356.5 3.2 copy-start.1
Sparse Core Ops, SparseCore 0:
  10.4 111.4 all-gather.1
  224.4 132.0 all-reduce.1
  366.3 66.0 reduce-scatter.1
where the time goes:
time: 442 us; the launch traced here: 441 us
  waiting for transfers between devices  304 us (69%)
  loops' own time  58.2 us (13%)
  local copies, waits for them, and re-layouts  36.9 us (8%)
  matrix products  18.1 us (4%)
  between operations  13.9 us (3%)
  other arithmetic  9.68 us (2%)
    psum x1, waiting for transfers between devices, shards(): lax.psum(head_term.astype(jnp.bfloat16), 'mp').astype(jnp.float32)  132 us
    all_gather x1, waiting for transfers between devices, shards(): shard_piece = lax.all_gather(prefix_kv, 'req', axis=1, tiled=True)  107 us
    reduce_scatter x1, waiting for transfers between devices, shards(): lax.psum_scatter(projected.astype(jnp.bfloat16), 'mp', scatter_dimension=...  63.9 us
    another operation x1, loops' own time, shards(): result = lax.fori_loop(0, block_total, fold_step, own_part)  50.1 us
    reshape x1, local copies, waits for them, and re-layouts, shards(): blocks_here = shard_piece.reshape(2, block_total, KB, head_count, DH)  12.5 us
    unnamed x17, local copies, waits for them, and re-layouts  11.3 us
    dynamic_slice x16, local copies, waits for them, and re-layouts, fold_step(): logical = prefix_owner[block_index]  9.59 us
  transfers between devices with their start and end apart: 3, of which 3 were waited for; matrix products, arithmetic and copies ran while one was open for 2% of the time, Pallas kernels for 0%

commit v1 on v0

--- a/solution.py
+++ b/solution.py
@@ -82,7 +82,9 @@
         False,
     )
     key_offsets = jnp.arange(KB)
-    shard_piece = lax.all_gather(prefix_kv, "req", axis=1, tiled=True)
+    shard_piece = jnp.concatenate(
+        lax.all_to_all(jnp.stack([prefix_kv] * lax.axis_size("req")), "req", 0, 0), axis=1
+    )
     block_total = shard_piece.shape[1] // KB
     blocks_here = shard_piece.reshape(2, block_total, KB, head_count, DH)
 

time: 442 us -> 516 us (1.17)
  waiting for transfers between devices: 304 us -> 373 us
  starting transfers between devices: 0.12 us -> 11.6 us
  local copies, waits for them, and re-layouts: 36.9 us -> 30.1 us
    all_to_all x0 -> x1, waiting for transfers between devices: none -> 179 us  [shards(): lax.all_to_all(jnp.stack([prefix_kv] * lax.axis_size('req')), 'req', 0, 0)]
    all_gather x1 -> x0, waiting for transfers between devices: 107 us -> none  [shards(): shard_piece = lax.all_gather(prefix_kv, 'req', axis=1, tiled=True)]
    reshape x1 -> x0, local copies, waits for them, and re-layouts: 12.5 us -> none  [shards(): blocks_here = shard_piece.reshape(2, block_total, KB, head_count, DH)]
    all_to_all x0 -> x1, starting transfers between devices: none -> 11.6 us  [shards(): lax.all_to_all(jnp.stack([prefix_kv] * lax.axis_size('req')), 'req', 0, 0)]
    unnamed x17 -> x26, local copies, waits for them, and re-layouts: 11.3 us -> 15 us
  transfers between devices with their start and end apart: 3 -> 3, of which waited for: 3 -> 3; matrix products, arithmetic and copies ran while one was open for 2% -> 1% of each run, Pallas kernels for 0% -> 0%
where the time goes in v1:
time: 516 us; the launch traced here: 515 us
  waiting for transfers between devices  373 us (72%)
  loops' own time  58.9 us (11%)
  local copies, waits for them, and re-layouts  30.1 us (6%)
  matrix products  17.3 us (3%)
  between operations  14.2 us (3%)
  starting transfers between devices  11.6 us (2%)
  other arithmetic  9.7 us (2%)
    all_to_all x1, waiting for transfers between devices, shards(): lax.all_to_all(jnp.stack([prefix_kv] * lax.axis_size('req')), 'req', 0, 0)  179 us
    psum x1, waiting for transfers between devices, shards(): lax.psum(head_term.astype(jnp.bfloat16), 'mp').astype(jnp.float32)  130 us
    reduce_scatter x1, waiting for transfers between devices, shards(): lax.psum_scatter(projected.astype(jnp.bfloat16), 'mp', scatter_dimension=...  63.8 us
    another operation x1, loops' own time, shards(): result = lax.fori_loop(0, block_total, fold_step, own_part)  51 us
    unnamed x26, local copies, waits for them, and re-layouts  15 us
    all_to_all x1, starting transfers between devices, shards(): lax.all_to_all(jnp.stack([prefix_kv] * lax.axis_size('req')), 'req', 0, 0)  11.6 us
  transfers between devices with their start and end apart: 3, of which 3 were waited for; matrix products, arithmetic and copies ran while one was open for 1% of the time, Pallas kernels for 0%

profile of v1, /device:TPU:6, one launch (start us, length us, event | category | flops | bytes accessed | tf_op | source)
XLA Modules:
  0.0 514.6 jit_solution(9502711887898466621)
XLA Ops:
  7.2 1.4 copy.41
  8.6 4.2 stack.2
  12.8 11.6 %all-to-all-start = ((bf16[16,2,512,256]{2,3,1,0:T(8,128)(2,1)}), bf16[16,2,512,256]{2,3,1,0:T(8,128)(2,1)}, u32[]{:S(2)}, u32[]{:S(2)}) async-start(bf16[16,2,512,256]{2,3,1,0:T(8,128)(2,1)} %stack.2), calls=%async_computation | async-start | bytes 16777216 | tf_op jit(solution)/shard_map/all_to_all | solution.py:86
  24.8 0.6 dynamic_slice.34
  25.4 0.6 iota_compare_fusion.1
  26.8 0.6 dynamic_slice.35
  27.6 179.4 %all-to-all-done = bf16[16,2,512,256]{2,3,1,0:T(8,128)(2,1)} async-done(((bf16[16,2,512,256]{2,3,1,0:T(8,128)(2,1)}), bf16[16,2,512,256]{2,3,1,0:T(8,128)(2,1)}, u32[]{:S(2)}, u32[]{:S(2)}) %all-to-all-start) | async-done | bytes 8388640 | tf_op jit(solution)/shard_map/all_to_all | solution.py:86
  207.0 11.9 %copy.45 = bf16[2,16,512,2,128]{4,2,3,1,0:T(8,128)(2,1)} copy(bf16[2,16,512,2,128]{2,4,3,0,1:T(8,128)(2,1)} %bitcast.26) | data formatting | bytes 16777216
  218.9 79.7 %while.20 = (s32[]{:T(128)}, f32[1,128,2,128]{1,3,2,0:T(8,128)S(1)}, f32[1,128,2]{1,2,0:T(2,128)S(1)}, f32[1,128,2]{1,2,0:T(2,128)S(1)}, s32[16]{0:T(128)S(1)}, ...) while((s32[]{:T(128)}, ...), condition=%wide.region_7.8_spmd.clone, body=%wide.region_2.7_spmd.clone.sunk | while | flops 68782248 | bytes 2980497 | solution.py:111
  226.5 4.7 conditional.3
  228.5 1.2 fusion.120
  229.9 1.3 fusion.10
  250.2 4.7 conditional.3
  252.3 1.2 fusion.120
  253.6 1.3 fusion.10
  254.9 0.6 dynamic_slice.54
  258.7 0.6 dynamic_slice.54
  266.3 4.7 conditional.3
  268.4 1.2 fusion.120
  269.7 1.3 fusion.10
  293.9 4.7 conditional.3
  295.9 1.2 fusion.120
  297.3 1.3 fusion.10
  299.5 1.2 convert_element_type.80
  300.7 129.6 %all-reduce.2.cloned.1.call-done = bf16[128,4096]{1,0:T(8,128)(2,1)} async-done(((bf16[128,4096]{1,0:T(8,128)(2,1)}), bf16[128,4096]{1,0:T(8,128)(2,1)}) %all-reduce.2.cloned.1.call-update) | async-done | bytes 1048592 | tf_op jit(solution)/shard_map/psum | solution.py:124
  430.3 1.5 convert_reduce_fusion
  431.9 1.7 multiply_reduce_fusion
  433.5 6.4 %convolution_convert_fusion = bf16[128,4096]{1,0:T(8,128)(2,1)} fusion(bf16[512,4096]{1,0:T(8,128)(2,1)} %param.22, bf16[4096,512]{1,0:T(8,128)(2,1)} %param.21, bf16[128,4096]{1,0:T(8,128)(2,1)S(1)} %copy-done.1, f32[4096]{0:T(1024)S(1)} %copy-done.5, f32[128]{0:T(128)S(1)} %add_rsqrt_fusion, f32[128]{0:T(128)S(1)} %broadcast_multiply_fusion), kind=kOutput, calls=%fused_computation.40 | convolution fusion | flops 1081147392 | bytes 10503168 | tf_op jit(solution)/shard_map/dot_general | solution.py:132
  440.0 0.7 copy.47
  440.8 1.5 convert_element_type.81
  442.3 63.8 %reduce-scatter.2.cloned.1.call-done = bf16[128,256]{1,0:T(8,128)(2,1)} async-done(((bf16[128,4096]{1,0:T(8,128)(2,1)}), bf16[128,256]{1,0:T(8,128)(2,1)}) %reduce-scatter.2.cloned.1.call-update) | async-done | bytes 65552 | tf_op jit(solution)/shard_map/reduce_scatter | solution.py:133
  506.1 1.7 select_convert_fusion
  (146 shorter events, 12.1 us)
Async XLA Ops:
  7.2 291.5 %copy-start = (bf16[256,4096]{1,0:T(8,128)(2,1)S(1)}, bf16[256,4096]{1,0:T(8,128)(2,1)}, u32[]{:S(2)}) copy-start(bf16[256,4096]{1,0:T(8,128)(2,1)} %param.20) | copy-start | bytes 6291460
  12.8 11.6 %copy-start.3 = (bf16[2,128,256]{2,1,0:T(8,128)(2,1)S(1)}, bf16[2,128,256]{2,1,0:T(8,128)(2,1)}, u32[]{:S(2)}) copy-start(bf16[2,128,256]{2,1,0:T(8,128)(2,1)} %param.16) | copy-start | bytes 393220
  12.8 11.9 %copy-start.2 = (bf16[128,256]{1,0:T(8,128)(2,1)S(1)}, bf16[128,256]{1,0:T(8,128)(2,1)}, u32[]{:S(2)}) copy-start(bf16[128,256]{1,0:T(8,128)(2,1)} %param.15) | copy-start | bytes 196612
  12.8 12.0 %copy-start.6 = (s32[16]{0:T(128)S(1)}, s32[16]{0:T(128)}, u32[]{:S(2)}) copy-start(s32[16]{0:T(128)} %param.23) | copy-start | bytes 196
  12.8 14.1 %copy-start.7 = (s32[16]{0:T(128)S(1)}, s32[16]{0:T(128)}, u32[]{:S(2)}) copy-start(s32[16]{0:T(128)} %param.24) | copy-start | bytes 196
  12.8 194.2 %all-to-all-start = ((bf16[16,2,512,256]{2,3,1,0:T(8,128)(2,1)}), bf16[16,2,512,256]{2,3,1,0:T(8,128)(2,1)}, u32[]{:S(2)}, u32[]{:S(2)}) async-start(bf16[16,2,512,256]{2,3,1,0:T(8,128)(2,1)} %stack.2), calls=%async_computation | async-start | bytes 16777216 | tf_op jit(solution)/shard_map/all_to_all | solution.py:86
  24.3 406.0 %all-reduce.2.cloned.1.call-start = ((), (), s32[]{:S(2)}) async-start(), calls=%async_computation.2 | async-start | bytes 2097152 | tf_op jit(solution)/shard_map/psum | solution.py:124
  207.0 11.9 %copy-start.8 = (s32[16]{0:T(128)S(1)}, s32[16]{0:T(128)}, u32[]{:S(2)}) copy-start(s32[16]{0:T(128)} %param.25) | copy-start | bytes 196
  298.6 0.8 copy-start.4
  300.7 132.9 %copy-start.5 = (f32[4096]{0:T(1024)S(1)}, f32[4096]{0:T(1024)}, u32[]{:S(2)}) copy-start(f32[4096]{0:T(1024)} %param.19) | copy-start | bytes 49156
  300.7 205.4 %reduce-scatter.2.cloned.1.call-start = ((), (), s32[]{:S(2)}) async-start(), calls=%async_computation.3 | async-start | bytes 1114112 | tf_op jit(solution)/shard_map/reduce_scatter | solution.py:133
  430.3 3.2 copy-start.1
Sparse Core Ops, SparseCore 0:
  300.8 129.4 all-reduce.1
  440.1 65.8 reduce-scatter.1
